TPU v7x, 256 devices: a whole 4x4x8 slice. The times are simulated.
256 devices in a mesh: sec: 2 (over y_lo), gx: 8 (over y_hi, x), gy: 16 (over z, core).
Axes of the slice: x: 4, y: 4 (y_hi: 2, y_lo: 2; y = y_hi * 2 + y_lo), z: 8, core: 2. Of those that a mesh axis runs over, the one named last changes fastest.
Arguments:
- state: float32 [2, 3, 8, 16, 102400], P('sec', None, 'gx', 'gy'), may hold values from -6 to 6
- previous: float32 [2, 3, 8, 16, 102400], P('sec', None, 'gx', 'gy'), may hold values from -6 to 6
- coeff: float32 [2, 2, 8, 16, 102400], P('sec', None, 'gx', 'gy'), may hold values from 0.04 to 0.16
- wet_mask: int32 [8, 16, 102400], P('gx', 'gy'), may hold values 0 or 1
- link_dest: int32 [2, 8, 16, 256, 1], P('sec', 'gx', 'gy'), may hold values from 0 to 127; in each aligned block of 256 rows (0 to 255, 256 to 511, ..., all dimensions but the last counted through in order) at most 4 rows name the same one
- link_rows: int32 [2, 8, 16, 256, 2], P('sec', 'gx', 'gy'), may hold values from 0 to 79, as said below
- link_weight: float32 [2, 8, 16, 256], P('sec', 'gx', 'gy'), may hold values from 0.5 to 2
Outputs:
- final_state: float32 [2, 3, 8, 16, 102400], P('sec', None, 'gx', 'gy')
Inputs may be any that keep to these rules, and one draw needn't show every extreme that they name: `link_rows`: in section 0, [..., 0] lies below 8 and [..., 1] below 80; in section 1, [..., 0] lies below 80 and [..., 1] below 8. `link_dest`: among the 256 links of one device at most 4 name the same owner.
All inputs are finite; a program needn't handle non-finite values. No bound on the sum of `wet_mask` on one device may be relied on, other than what follows from the above.
Results may differ from a plain program's by a relative error of at most 0.0001.
Values sent between devices are 32-bit elements; how exact they have to be, the bound alone decides.
A program may use at most 128 MiB of HBM per device.

v0:
```python
import functools

import jax
import jax.numpy as jnp
from jax import lax
from jax.experimental import pallas as pl
from jax.experimental.pallas import tpu as pltpu
from jax.sharding import PartitionSpec as P

CX = 8
CY = 128
REFINE = 10
NL = 100
STEPS = 4
CAP = 4

ROWS = CX * NL
BASE = 104
PAD_ROWS = BASE + ROWS + NL + 8
CHUNK = 40
EDGE = 16


def from_partner(value, axis, stride):
    return lax.ppermute(value, axis, [(i, i ^ 1 << stride) for i in range(lax.axis_size(axis))])


def shift_pairs(axis):
    count = lax.axis_size(axis)
    forward = [(i, i + 1) for i in range(count - 1)]
    backward = [(target, source) for source, target in forward]
    return forward, backward


def exchange_halos(current):
    forward_x, backward_x = shift_pairs("gx")
    forward_y, backward_y = shift_pairs("gy")
    low_x = lax.ppermute(current[:, ROWS - NL :], "gx", forward_x)
    high_x = lax.ppermute(current[:, :NL], "gx", backward_x)
    low_y = lax.ppermute(current[:, :, CY - 1 :], "gy", forward_y)
    high_y = lax.ppermute(current[:, :, :1], "gy", backward_y)
    return low_x, high_x, low_y, high_y


def fill_scratch(scratch, cur_ref, low_ref, high_ref, fields):
    for f in range(fields):
        scratch[f, pl.ds(BASE - NL, NL), :] = low_ref[f]
        scratch[f, pl.ds(BASE, ROWS), :] = cur_ref[f]
        scratch[f, pl.ds(BASE + ROWS, NL), :] = high_ref[f]


def lane_index(rows):
    return lax.broadcasted_iota(jnp.int32, (rows, CY), 1)


def row_mask(r0, rows, period, phase):
    local = lax.broadcasted_iota(jnp.int32, (rows, CY), 0)
    mask = jnp.zeros((rows, CY), jnp.bool_)
    for r in range(rows):
        if (r0 + r) % period == phase:
            mask = mask | (local == r)
    return mask


def exact_dot(a, b):
    return jnp.dot(a, b, precision=lax.Precision.HIGHEST, preferred_element_type=jnp.float32)


def landing_sum(rows_ref, arrived_ref, count):
    slots = rows_ref.shape[1]
    one_hot = (lax.broadcasted_iota(jnp.int32, (count, slots), 0) == rows_ref[...]).astype(jnp.float32)
    return exact_dot(one_hot, arrived_ref[...])


def spread(cb):
    coarse = lax.broadcasted_iota(jnp.int32, (CY, CY), 0)
    fine = lax.broadcasted_iota(jnp.int32, (CY, CY), 1) + cb * CY
    return ((fine >= coarse * REFINE) & (fine < coarse * REFINE + REFINE)).astype(jnp.float32)


def elastic_kernel(cur_ref, prev_ref, coef_ref, low_ref, high_ref, left_ref, right_ref, rows_ref, arrived_ref,
                   pick_ref, out_ref, tiles_ref, scratch):
    fill_scratch(scratch, cur_ref, low_ref, high_ref, 3)
    force = landing_sum(rows_ref, arrived_ref, CX)
    lanes = lane_index(CHUNK)
    first_lane = lanes == 0
    last_lane = lanes == CY - 1
    own_axis = (0, 2, 1)
    for r0 in range(0, ROWS, CHUNK):
        top_layer = row_mask(r0, CHUNK, NL, 0)
        bottom_layer = row_mask(r0, CHUNK, NL, NL - 1)
        shear = coef_ref[0, pl.ds(r0, CHUNK), :]
        lame = coef_ref[1, pl.ds(r0, CHUNK), :]
        stiffness = lame + 2.0 * shear
        for c in range(3):
            at = BASE + r0
            v = scratch[c, pl.ds(at, CHUNK), :]
            along_first = scratch[c, pl.ds(at + NL, CHUNK), :] - 2.0 * v + scratch[c, pl.ds(at - NL, CHUNK), :]
            deeper = jnp.where(bottom_layer, 0.0, scratch[c, pl.ds(at + 1, CHUNK), :])
            shallower = jnp.where(top_layer, 0.0, scratch[c, pl.ds(at - 1, CHUNK), :])
            along_depth = deeper - 2.0 * v + shallower
            after = jnp.where(last_lane, right_ref[c, pl.ds(r0, CHUNK), :], pltpu.roll(v, CY - 1, 1))
            before = jnp.where(first_lane, left_ref[c, pl.ds(r0, CHUNK), :], pltpu.roll(v, 1, 1))
            along_second = after - 2.0 * v + before
            factors = [stiffness if own_axis[c] == axis_index else shear for axis_index in range(3)]
            acceleration = factors[0] * along_first + factors[1] * along_depth + factors[2] * along_second
            out_ref[c, pl.ds(r0, CHUNK), :] = 2.0 * v - prev_ref[c, pl.ds(r0, CHUNK), :] + acceleration
    for x in range(CX):
        out_ref[2, pl.ds(x * NL, 1), :] = out_ref[2, pl.ds(x * NL, 1), :] + force[x : x + 1]
    uplift = out_ref[2, pl.ds(0, CX, stride=NL), :]
    tiles_ref[...] = exact_dot(pick_ref[:, :CX], uplift)


def shallow_kernel(cur_ref, prev_ref, coef_ref, wet_ref, low_ref, high_ref, left_ref, right_ref, rows_ref, arrived_ref,
                   pick_ref, out_ref, tiles_ref, scratch, source_ref, left_pad, right_pad):
    fill_scratch(scratch, cur_ref, low_ref, high_ref, 3)
    for f in range(3):
        left_pad[f, pl.ds(EDGE, ROWS), :] = left_ref[f]
        right_pad[f, pl.ds(EDGE, ROWS), :] = right_ref[f]
    coarse_source = landing_sum(rows_ref, arrived_ref, REFINE * CX)
    for cb in range(REFINE):
        source_ref[pl.ds(cb, REFINE * CX, stride=REFINE), :] = exact_dot(coarse_source, spread(cb))
    lanes = lane_index(CHUNK)
    first_lane = lanes == 0
    last_lane = lanes == CY - 1
    first_block = row_mask(0, CHUNK, REFINE, 0)
    last_block = row_mask(0, CHUNK, REFINE, REFINE - 1)
    for r0 in range(0, ROWS, CHUNK):
        at = BASE + r0

        def rows_diff(f):
            return scratch[f, pl.ds(at + REFINE, CHUNK), :] - scratch[f, pl.ds(at - REFINE, CHUNK), :]

        def columns_diff(f):
            v = scratch[f, pl.ds(at, CHUNK), :]
            wrap_after = jnp.where(last_block, right_pad[f, pl.ds(EDGE + r0 - (REFINE - 1), CHUNK), :],
                                   pltpu.roll(scratch[f, pl.ds(at + 1, CHUNK), :], CY - 1, 1))
            wrap_before = jnp.where(first_block, left_pad[f, pl.ds(EDGE + r0 + REFINE - 1, CHUNK), :],
                                    pltpu.roll(scratch[f, pl.ds(at - 1, CHUNK), :], 1, 1))
            after = jnp.where(last_lane, wrap_after, pltpu.roll(v, CY - 1, 1))
            before = jnp.where(first_lane, wrap_before, pltpu.roll(v, 1, 1))
            return after - before

        wave = coef_ref[0, pl.ds(r0, CHUNK), :]
        area = coef_ref[1, pl.ds(r0, CHUNK), :]
        wet = wet_ref[pl.ds(r0, CHUNK), :].astype(jnp.float32)
        eta_r = rows_diff(0)
        eta_c = columns_diff(0)
        out_ref[1, pl.ds(r0, CHUNK), :] = wet * (prev_ref[1, pl.ds(r0, CHUNK), :] - wave * eta_r)
        out_ref[2, pl.ds(r0, CHUNK), :] = wet * (prev_ref[2, pl.ds(r0, CHUNK), :] - wave * eta_c)
        divergence = rows_diff(1) + columns_diff(2)
        out_ref[0, pl.ds(r0, CHUNK), :] = wet * (
            prev_ref[0, pl.ds(r0, CHUNK), :] - area * divergence + source_ref[pl.ds(r0, CHUNK), :]
        )
    total = jnp.zeros((REFINE * CX, CY), jnp.float32)
    for cb in range(REFINE):
        total = total + exact_dot(out_ref[0, pl.ds(cb, REFINE * CX, stride=REFINE), :], spread(cb).T)
    tiles_ref[...] = exact_dot(pick_ref[...], total / REFINE)


def vmem_specs(count):
    return [pl.BlockSpec(memory_space=pltpu.VMEM)] * count


def run_step(kernel, scratch_shapes, *operands):
    slots = operands[-1].shape[0]
    return pl.pallas_call(
        kernel,
        out_shape=(
            jax.ShapeDtypeStruct((3, ROWS, CY), jnp.float32),
            jax.ShapeDtypeStruct((slots, CY), jnp.float32),
        ),
        in_specs=vmem_specs(len(operands)),
        out_specs=tuple(vmem_specs(2)),
        scratch_shapes=scratch_shapes,
    )(*operands)


def exchange_kernel(sizes, out_ref, in_ref, land, send_sem, recv_sem):
    owners, columns = sizes
    other = 1 - lax.axis_index("sec")
    me = lax.axis_index("gx") * columns + lax.axis_index("gy")
    barrier = pltpu.get_barrier_semaphore()

    def greet(d, carry):
        pl.semaphore_signal(barrier, inc=1, device_id=(other, d // columns, d % columns),
                            device_id_type=pl.DeviceIdType.MESH)
        return carry

    lax.fori_loop(0, owners, greet, 0)
    pl.semaphore_wait(barrier, owners)

    def send(d, carry):
        pltpu.make_async_remote_copy(
            src_ref=out_ref.at[pl.ds(d * CAP, CAP)],
            dst_ref=land.at[pl.ds(me * CAP, CAP)],
            send_sem=send_sem,
            recv_sem=recv_sem,
            device_id=(other, d // columns, d % columns),
            device_id_type=pl.DeviceIdType.MESH,
        ).start()
        return carry

    lax.fori_loop(0, owners, send, 0)
    whole = pltpu.make_async_remote_copy(
        src_ref=out_ref,
        dst_ref=land,
        send_sem=send_sem,
        recv_sem=recv_sem,
        device_id=(other, lax.axis_index("gx"), lax.axis_index("gy")),
        device_id_type=pl.DeviceIdType.MESH,
    )
    whole.wait_send()
    whole.wait_recv()
    in_ref[...] = land[...]


def exchange_tiles(outgoing, owners, columns):
    return pl.pallas_call(
        functools.partial(exchange_kernel, (owners, columns)),
        out_shape=jax.ShapeDtypeStruct(outgoing.shape, jnp.float32),
        in_specs=vmem_specs(1),
        out_specs=pl.BlockSpec(memory_space=pltpu.VMEM),
        scratch_shapes=[
            pltpu.VMEM(outgoing.shape, jnp.float32),
            pltpu.SemaphoreType.DMA(()),
            pltpu.SemaphoreType.DMA(()),
        ],
        compiler_params=pltpu.CompilerParams(collective_id=0, has_side_effects=True),
    )(outgoing)


def route(payload):
    tile_data, tile_rows = payload
    width = tile_data.shape[-1]
    received_data, received_rows = (
        lax.all_to_all(tile_data, ("gx", "gy"), split_axis=0, concat_axis=0, tiled=True),
        lax.all_to_all(tile_rows, ("gx", "gy"), split_axis=0, concat_axis=0, tiled=True),
    )
    return (received_data.reshape(-1, width), received_rows.reshape(-1))


def deliver(outgoing, send_rows):
    routed = route((outgoing, send_rows))
    return from_partner((routed[0], routed[1]), "sec", 0)


def on_device(state, previous, coeff, wet_mask, link_dest, link_rows, link_weight):
    section = lax.axis_index("sec")
    owners = lax.axis_size("gx") * lax.axis_size("gy")
    fine_rows = REFINE * CX
    fine_cols = REFINE * CY
    current = state[0, :, 0, 0].reshape(3, ROWS, CY)
    earlier = previous[0, :, 0, 0].reshape(3, ROWS, CY)
    factors = coeff[0, :, 0, 0].reshape(2, ROWS, CY)
    wet = wet_mask[0, 0].reshape(ROWS, CY)
    targets = link_dest.reshape(-1)
    pairs = link_rows.reshape(-1, 2)
    source_rows = pairs[:, 0]
    landing = pairs[:, 1]
    weights = link_weight.reshape(-1)
    one_hot = (targets[:, None] == jnp.arange(owners, dtype=jnp.int32)[None, :]).astype(jnp.int32)
    before = jnp.cumsum(one_hot, axis=0) - one_hot
    slot_index = jnp.sum(before * one_hot, axis=1)
    position = targets * CAP + slot_index
    send_rows = jnp.zeros((owners * CAP,), jnp.int32).at[position].set(landing).reshape(owners, CAP)
    slot_rows = jnp.full((owners * CAP,), -1, jnp.int32).at[position].set(source_rows)
    slot_weights = jnp.zeros((owners * CAP,), jnp.float32).at[position].set(weights)
    pick = jnp.where(slot_rows[:, None] == jnp.arange(fine_rows, dtype=jnp.int32)[None, :], slot_weights[:, None], 0.0)

    def elastic_rows():
        return current[2].reshape(CX, NL, CY)[:, 0, :][source_rows]

    def shallow_rows():
        picked_fine = current[0].reshape(fine_rows, fine_cols)[source_rows]
        return jnp.sum(picked_fine.reshape(-1, CY, REFINE), axis=-1) / REFINE

    picked = lax.cond(section == 0, elastic_rows, shallow_rows)
    outgoing = jnp.zeros((owners * CAP, CY), jnp.float32).at[position].set(picked * weights[:, None])
    arrived_rows = deliver(jnp.zeros((owners, CAP, CY), jnp.float32), send_rows)[1].reshape(1, -1)
    for step_index in range(STEPS):
        low_x, high_x, low_y, high_y = exchange_halos(current)
        arrived = exchange_tiles(outgoing, owners, lax.axis_size("gy"))

        def elastic_branch():
            scratch = [pltpu.VMEM((3, PAD_ROWS, CY), jnp.float32)]
            return run_step(elastic_kernel, scratch, current, earlier, factors, low_x, high_x, low_y, high_y,
                            arrived_rows, arrived, pick)

        def shallow_branch():
            scratch = [
                pltpu.VMEM((3, PAD_ROWS, CY), jnp.float32),
                pltpu.VMEM((ROWS, CY), jnp.float32),
                pltpu.VMEM((3, ROWS + 2 * EDGE, 1), jnp.float32),
                pltpu.VMEM((3, ROWS + 2 * EDGE, 1), jnp.float32),
            ]
            return run_step(shallow_kernel, scratch, current, earlier, factors, wet, low_x, high_x, low_y, high_y,
                            arrived_rows, arrived, pick)

        updated, outgoing = lax.cond(section == 0, elastic_branch, shallow_branch)
        earlier, current = (current, updated)
    return current.reshape(1, 3, 1, 1, -1)


def solution(mesh):
    placed = (
        P("sec", None, "gx", "gy", None),
        P("sec", None, "gx", "gy", None),
        P("sec", None, "gx", "gy", None),
        P("gx", "gy", None),
        P("sec", "gx", "gy", None, None),
        P("sec", "gx", "gy", None, None),
        P("sec", "gx", "gy", None),
    )
    return jax.shard_map(
        on_device,
        mesh=mesh,
        in_specs=placed,
        out_specs=P("sec", None, "gx", "gy", None),
        check_vma=False,
    )
```

profile of v0, /device:TPU:31, one launch (start us, length us, event | category | flops | bytes accessed | tf_op | source)
XLA Modules:
  0.0 230.6 jit_solution(3962664137246210772)
XLA Ops:
  5.6 16.1 %all-to-all-start = ((s32[128,1,4]{2,1,0:T(1,128)}), s32[128,1,4]{2,1,0:T(1,128)S(1)}, u32[]{:S(2)}, u32[]{:S(2)}) async-start(s32[128,1,4]{2,1,0:T(1,128)} %bitcast.17), calls=%async_computation | async-start | bytes 131072 | tf_op jit(solution)/shard_map/all_to_all | solution.py:238
  21.7 1.7 fusion.23
  23.4 3.0 %collective-permute-start.1 = (f32[3,100,128]{2,1,0:T(8,128)}, f32[3,100,128]{2,1,0:T(8,128)}, u32[]{:S(2)}, u32[]{:S(2)}) collective-permute-start(f32[3,100,128]{2,1,0:T(8,128)} %get-tuple-element.478), channel_id=1, source_target_pairs={{16,0},{32,16},{48,32},{64,48},{80,64},{96,80},{112,96},{17,1},{33... | collective-permute-start | bytes 460808 | tf_op jit(solution)/shard_map/ppermute | solution.py:39
  29.2 2.3 %copy.60 = f32[3,800,1]{1,2,0:T(1,128)} copy(f32[3,800,1]{2,1,0:T(8,128)} %get-tuple-element.477) | data formatting | bytes 19200 | tf_op jit(solution)/shard_map/slice | solution.py:40
  31.5 3.6 %collective-permute-start.2 = (f32[3,800,1]{1,2,0:T(1,128)}, f32[3,800,1]{1,2,0:T(1,128)S(1)}, u32[]{:S(2)}, u32[]{:S(2)}) collective-permute-start(f32[3,800,1]{1,2,0:T(1,128)} %copy.60), channel_id=1, source_target_pairs={{0,1},{1,2},{2,3},{3,4},{4,5},{5,6},{6,7},{7,8},{8,9},{9,10},{10,1... | collective-permute-start | bytes 28808 | tf_op jit(solution)/shard_map/ppermute | solution.py:40
  36.1 1.9 collective-permute-start.3
  38.1 1.6 scatter_custom_fusion.3
  43.3 10.7 %conditional.5 = (f32[256,128]{1,0:T(8,128)S(1)}) conditional(s32[]{:T(128)} %convert_element_type.14, (f32[3,800,128]{2,1,0:T(8,128)S(1)}, s32[256]{0:T(256)}) %tuple.127, (f32[3,800,128]{2,1,0:T(8,128)S(1)}, s32[256]{0:T(256)}) %tuple.128), branch_computations={%region_4.6_spmd, %region_6.7_spmd} | conditional | flops 329472 | bytes 11477004 | solution.py:278
  44.1 2.3 gather_fusion
  46.4 2.8 %copy.57 = f32[256,1280]{0,1:T(8,128)} copy(f32[256,1280]{1,0:T(8,128)} %gather_fusion) | data formatting | bytes 2621440 | tf_op jit(solution)/shard_map/cond/branch_0_fun/gather | solution.py:275
  49.2 2.6 %reshape.64 = f32[256,128,10]{0,2,1:T(8,128)} reshape(f32[256,1280]{0,1:T(8,128)} %copy.57) | data formatting | bytes 2621440 | tf_op jit(solution)/shard_map/cond/branch_0_fun/reshape | solution.py:276
  51.8 2.0 reduce_sum.9
  54.0 2.1 scatter_custom_fusion.1.out_ref
  56.0 24.1 %shard_map.75 = f32[512,128]{1,0:T(8,128)} custom-call(f32[512,128]{1,0:T(8,128)} %scatter_custom_fusion.1.out_ref), custom_call_target="tpu_custom_call" | custom-call | tf_op jit(solution)/shard_map/pallas_call | solution.py:219
  80.2 9.6 %conditional.6 = ((f32[3,800,128]{2,1,0:T(8,128)S(1)}, f32[512,128]{1,0:T(8,128)})) conditional(s32[]{:T(128)} %convert_element_type.14, (f32[3,800,128]{2,1,0:T(8,128)S(1)}, f32[3,800,128]{2,1,0:T(8,128)}, f32[2,800,128]{2,1,0:T(8,128)S(1)}, s32[800,128]{1,0:T(8,128)}, f32[3,100,128]{2,1,0:T(8,128)}, /*index=5*/f32[3,100,128]{2,1,0:T(8,128)}, ...), branch_computations={%region_10.11_spmd, %region_11.12_spmd} | conditional | bytes 38408 | solution.py:300
  80.4 1.5 copy.67.right_ref
  81.8 1.4 copy.66.left_ref
  83.3 6.5 %branch_0_fun.4 = (f32[3,800,128]{2,1,0:T(8,128)S(1)}, f32[512,128]{1,0:T(8,128)}) custom-call(f32[3,800,128]{2,1,0:T(8,128)S(1)} %get-tuple-element.191.cur_ref, f32[3,800,128]{2,1,0:T(8,128)} %get-tuple-element.192.prev_ref, f32[2,800,128]{2,1,0:T(8,128)S(1)} %get-tuple-element.193.coef_ref, s32[800,128]{1,0:T(8,128)} %get-tuple-element.194.wet_ref, ...), custom_call_target="tpu_custom_call" | custom-call | tf_op jit(solution)/shard_map/cond/branch_0_fun/pallas_call | solution.py:167
  90.5 1.5 copy.70
  92.0 2.2 collective-permute-start.6
  95.5 1.5 fusion.18
  97.0 2.6 %collective-permute-start.8 = (f32[3,800,1]{1,2,0:T(1,128)}, f32[3,800,1]{1,2,0:T(1,128)S(1)}, u32[]{:S(2)}, u32[]{:S(2)}) collective-permute-start(f32[3,800,1]{1,2,0:T(1,128)} %get-tuple-element.468), channel_id=1, source_target_pairs={{1,0},{2,1},{3,2},{4,3},{5,4},{6,5},{7,6},{8,7},{9,8},{10,9},{11,1... | collective-permute-start | bytes 28808 | tf_op jit(solution)/shard_map/ppermute | solution.py:41
  99.6 3.1 %collective-permute-start.7 = (f32[3,800,1]{1,2,0:T(1,128)}, f32[3,800,1]{1,2,0:T(1,128)}, u32[]{:S(2)}, u32[]{:S(2)}) collective-permute-start(f32[3,800,1]{1,2,0:T(1,128)} %get-tuple-element.469), channel_id=1, source_target_pairs={{0,1},{1,2},{2,3},{3,4},{4,5},{5,6},{6,7},{7,8},{8,9},{9,10},{10,1... | collective-permute-start | bytes 28808 | tf_op jit(solution)/shard_map/ppermute | solution.py:40
  102.7 22.6 %shard_map.76 = f32[512,128]{1,0:T(8,128)} custom-call(f32[512,128]{1,0:T(8,128)} %get-tuple-element.284.out_ref), custom_call_target="tpu_custom_call" | custom-call | tf_op jit(solution)/shard_map/pallas_call | solution.py:219
  125.4 9.7 %conditional.7 = ((f32[3,800,128]{2,1,0:T(8,128)}, f32[512,128]{1,0:T(8,128)})) conditional(s32[]{:T(128)} %convert_element_type.14, (f32[3,800,128]{2,1,0:T(8,128)S(1)}, f32[3,800,128]{2,1,0:T(8,128)S(1)}, f32[2,800,128]{2,1,0:T(8,128)S(1)}, s32[800,128]{1,0:T(8,128)}, f32[3,100,128]{2,1,0:T(8,128)}, /*index=5*/f32[3,100,128]{2,1,0:T(8,128)}, ...), branch_computations={%region_12.13_spmd, %region_13.14_spmd} | conditional | bytes 38408 | solution.py:300
  126.8 2.2 copy.72.left_ref
  129.0 6.1 %branch_0_fun.5 = (f32[3,800,128]{2,1,0:T(8,128)}, f32[512,128]{1,0:T(8,128)}) custom-call(f32[3,800,128]{2,1,0:T(8,128)S(1)} %get-tuple-element.212.cur_ref, f32[3,800,128]{2,1,0:T(8,128)S(1)} %get-tuple-element.213.prev_ref, f32[2,800,128]{2,1,0:T(8,128)S(1)} %get-tuple-element.214.coef_ref, s32[800,128]{1,0:T(8,128)} %get-tuple-element.215.wet_ref, ...), custom_call_target="tpu_custom_call" | custom-call | tf_op jit(solution)/shard_map/cond/branch_0_fun/pallas_call | solution.py:167
  135.1 1.7 fusion.20
  136.8 2.9 %copy.76 = f32[3,800,128]{1,2,0:T(8,128)} copy(f32[3,800,128]{2,1,0:T(8,128)} %get-tuple-element.285) | data formatting | bytes 2457600 | tf_op jit(solution)/shard_map/cond | solution.py:300
  139.8 2.1 collective-permute-start.10
  143.1 1.5 fusion.17
  144.7 2.6 %collective-permute-start.12 = (f32[3,800,1]{1,2,0:T(1,128)}, f32[3,800,1]{1,2,0:T(1,128)S(1)}, u32[]{:S(2)}, u32[]{:S(2)}) collective-permute-start(f32[3,800,1]{1,2,0:T(1,128)} %get-tuple-element.466), channel_id=1, source_target_pairs={{1,0},{2,1},{3,2},{4,3},{5,4},{6,5},{7,6},{8,7},{9,8},{10,9},{11,1... | collective-permute-start | bytes 28808 | tf_op jit(solution)/shard_map/ppermute | solution.py:41
  147.3 3.2 %collective-permute-start.11 = (f32[3,800,1]{1,2,0:T(1,128)}, f32[3,800,1]{1,2,0:T(1,128)}, u32[]{:S(2)}, u32[]{:S(2)}) collective-permute-start(f32[3,800,1]{1,2,0:T(1,128)} %get-tuple-element.467), channel_id=1, source_target_pairs={{0,1},{1,2},{2,3},{3,4},{4,5},{5,6},{6,7},{7,8},{8,9},{9,10},{10,1... | collective-permute-start | bytes 28808 | tf_op jit(solution)/shard_map/ppermute | solution.py:40
  150.4 22.6 %shard_map.77 = f32[512,128]{1,0:T(8,128)} custom-call(f32[512,128]{1,0:T(8,128)} %get-tuple-element.286.out_ref), custom_call_target="tpu_custom_call" | custom-call | tf_op jit(solution)/shard_map/pallas_call | solution.py:219
  173.1 9.9 %conditional.8 = ((f32[3,800,128]{2,1,0:T(8,128)}, f32[512,128]{1,0:T(8,128)})) conditional(s32[]{:T(128)} %convert_element_type.14, (f32[3,800,128]{2,1,0:T(8,128)S(1)}, f32[3,800,128]{2,1,0:T(8,128)S(1)}, f32[2,800,128]{2,1,0:T(8,128)S(1)}, s32[800,128]{1,0:T(8,128)}, f32[3,100,128]{2,1,0:T(8,128)}, /*index=5*/f32[3,100,128]{2,1,0:T(8,128)}, ...), branch_computations={%region_14.15_spmd, %region_15.16_spmd} | conditional | bytes 38408 | solution.py:300
  173.3 1.4 copy.79.right_ref
  174.8 2.2 copy.78.left_ref
  176.9 6.1 %branch_0_fun.6 = (f32[3,800,128]{2,1,0:T(8,128)}, f32[512,128]{1,0:T(8,128)}) custom-call(f32[3,800,128]{2,1,0:T(8,128)S(1)} %get-tuple-element.233.cur_ref, f32[3,800,128]{2,1,0:T(8,128)S(1)} %get-tuple-element.234.prev_ref, f32[2,800,128]{2,1,0:T(8,128)S(1)} %get-tuple-element.235.coef_ref, s32[800,128]{1,0:T(8,128)} %get-tuple-element.236.wet_ref, ...), custom_call_target="tpu_custom_call" | custom-call | tf_op jit(solution)/shard_map/cond/branch_0_fun/pallas_call | solution.py:167
  183.0 1.7 fusion.19
  184.8 2.9 %copy.82 = f32[3,800,128]{1,2,0:T(8,128)} copy(f32[3,800,128]{2,1,0:T(8,128)} %get-tuple-element.287) | data formatting | bytes 2457600 | tf_op jit(solution)/shard_map/cond | solution.py:300
  187.7 2.0 collective-permute-start.14
  191.0 1.5 fusion.16
  192.6 2.6 %collective-permute-start.16 = (f32[3,800,1]{1,2,0:T(1,128)}, f32[3,800,1]{1,2,0:T(1,128)S(1)}, u32[]{:S(2)}, u32[]{:S(2)}) collective-permute-start(f32[3,800,1]{1,2,0:T(1,128)} %get-tuple-element.464), channel_id=1, source_target_pairs={{1,0},{2,1},{3,2},{4,3},{5,4},{6,5},{7,6},{8,7},{9,8},{10,9},{11,1... | collective-permute-start | bytes 28808 | tf_op jit(solution)/shard_map/ppermute | solution.py:41
  195.2 3.2 %collective-permute-start.15 = (f32[3,800,1]{1,2,0:T(1,128)}, f32[3,800,1]{1,2,0:T(1,128)}, u32[]{:S(2)}, u32[]{:S(2)}) collective-permute-start(f32[3,800,1]{1,2,0:T(1,128)} %get-tuple-element.465), channel_id=1, source_target_pairs={{0,1},{1,2},{2,3},{3,4},{4,5},{5,6},{6,7},{7,8},{8,9},{9,10},{10,1... | collective-permute-start | bytes 28808 | tf_op jit(solution)/shard_map/ppermute | solution.py:40
  198.3 22.6 %shard_map.78 = f32[512,128]{1,0:T(8,128)} custom-call(f32[512,128]{1,0:T(8,128)} %get-tuple-element.288.out_ref), custom_call_target="tpu_custom_call" | custom-call | tf_op jit(solution)/shard_map/pallas_call | solution.py:219
  220.9 9.7 %conditional.9 = (f32[1,3,1,1,102400]{4,3,2,1,0:T(1,128)}) conditional(s32[]{:T(128)} %convert_element_type.14, (f32[3,800,128]{2,1,0:T(8,128)S(1)}, f32[3,800,128]{2,1,0:T(8,128)S(1)}, f32[2,800,128]{2,1,0:T(8,128)S(1)}, s32[800,128]{1,0:T(8,128)}, f32[3,100,128]{2,1,0:T(8,128)}, /*index=5*/f32[3,100,128]{2,1,0:T(8,128)}, ...), branch_computations={%region_16.17_spmd, %region_17.18_spmd} | conditional | bytes 38408 | solution.py:300
  222.4 2.2 copy.84.left_ref
  224.6 6.1 %branch_0_fun.7 = (f32[3,800,128]{2,1,0:T(8,128)}, f32[512,128]{1,0:T(8,128)}) custom-call(f32[3,800,128]{2,1,0:T(8,128)S(1)} %get-tuple-element.254.cur_ref, f32[3,800,128]{2,1,0:T(8,128)S(1)} %get-tuple-element.255.prev_ref, f32[2,800,128]{2,1,0:T(8,128)S(1)} %get-tuple-element.256.coef_ref, s32[800,128]{1,0:T(8,128)} %get-tuple-element.257.wet_ref, ...), custom_call_target="tpu_custom_call" | custom-call | tf_op jit(solution)/shard_map/cond/branch_0_fun/pallas_call | solution.py:167
  (66 shorter events, 21.3 us)
Async XLA Ops:
  0.0 27.8 %copy-start = (f32[1,3,1,1,102400]{4,3,2,1,0:T(1,128)S(1)}, f32[1,3,1,1,102400]{4,3,2,1,0:T(1,128)}, u32[]{:S(2)}) copy-start(f32[1,3,1,1,102400]{4,3,2,1,0:T(1,128)} %param.17) | copy-start | bytes 3686404
  0.8 38.8 %copy-start.4 = (s32[256,1]{0,1:T(1,128)}, s32[256,1]{0,1:T(1,128)S(1)}, u32[]{:S(2)}) copy-start(s32[256,1]{0,1:T(1,128)S(1)} %get-tuple-element.480) | copy-start | bytes 3076
  3.4 36.2 %copy-start.6 = (s32[256,1]{0,1:T(1,128)}, s32[256,1]{0,1:T(1,128)S(1)}, u32[]{:S(2)}) copy-start(s32[256,1]{0,1:T(1,128)S(1)} %compare_select_fusion.2) | copy-start | bytes 3076
  5.6 35.5 %all-to-all-start = ((s32[128,1,4]{2,1,0:T(1,128)}), s32[128,1,4]{2,1,0:T(1,128)S(1)}, u32[]{:S(2)}, u32[]{:S(2)}) async-start(s32[128,1,4]{2,1,0:T(1,128)} %bitcast.17), calls=%async_computation | async-start | bytes 131072 | tf_op jit(solution)/shard_map/all_to_all | solution.py:238
  23.4 56.7 %collective-permute-start.1 = (f32[3,100,128]{2,1,0:T(8,128)}, f32[3,100,128]{2,1,0:T(8,128)}, u32[]{:S(2)}, u32[]{:S(2)}) collective-permute-start(f32[3,100,128]{2,1,0:T(8,128)} %get-tuple-element.478), channel_id=1, source_target_pairs={{16,0},{32,16},{48,32},{64,48},{80,64},{96,80},{112,96},{17,1},{33... | collective-permute-start | bytes 460808 | tf_op jit(solution)/shard_map/ppermute | solution.py:39
  26.5 53.7 %collective-permute-start = (f32[3,100,128]{2,1,0:T(8,128)}, f32[3,100,128]{2,1,0:T(8,128)}, u32[]{:S(2)}, u32[]{:S(2)}) collective-permute-start(f32[3,100,128]{2,1,0:T(8,128)} %get-tuple-element.479), channel_id=1, source_target_pairs={{0,16},{16,32},{32,48},{48,64},{64,80},{80,96},{96,112},{1,17},{17... | collective-permute-start | bytes 460808 | tf_op jit(solution)/shard_map/ppermute | solution.py:38
  31.5 48.6 %collective-permute-start.2 = (f32[3,800,1]{1,2,0:T(1,128)}, f32[3,800,1]{1,2,0:T(1,128)S(1)}, u32[]{:S(2)}, u32[]{:S(2)}) collective-permute-start(f32[3,800,1]{1,2,0:T(1,128)} %copy.60), channel_id=1, source_target_pairs={{0,1},{1,2},{2,3},{3,4},{4,5},{5,6},{6,7},{7,8},{8,9},{9,10},{10,1... | collective-permute-start | bytes 28808 | tf_op jit(solution)/shard_map/ppermute | solution.py:40
  36.1 44.0 %collective-permute-start.3 = (f32[3,800,1]{1,2,0:T(1,128)}, f32[3,800,1]{1,2,0:T(1,128)S(1)}, u32[]{:S(2)}, u32[]{:S(2)}) collective-permute-start(f32[3,800,1]{1,2,0:T(1,128)} %copy.61), channel_id=1, source_target_pairs={{1,0},{2,1},{3,2},{4,3},{5,4},{6,5},{7,6},{8,7},{9,8},{10,9},{11,1... | collective-permute-start | bytes 28808 | tf_op jit(solution)/shard_map/ppermute | solution.py:41
  42.5 37.6 %collective-permute-start.4 = (s32[512]{0:T(512)S(1)}, s32[512]{0:T(512)S(1)}, u32[]{:S(2)}, u32[]{:S(2)}) collective-permute-start(s32[512]{0:T(512)S(1)} %reshape.72), channel_id=1, source_target_pairs={{0,128},{128,0},{1,129},{129,1},{2,130},{130,2},{3,131},{131,3},{4... | collective-permute-start | bytes 6152 | tf_op jit(solution)/shard_map/ppermute | solution.py:25
  43.2 10.7 %copy-start.5 = (f32[1,1,1,256]{3,2,1,0:T(1,128)S(1)}, f32[1,1,1,256]{3,2,1,0:T(1,128)}, u32[]{:S(2)}) copy-start(f32[1,1,1,256]{3,2,1,0:T(1,128)} %param.23) | copy-start | bytes 3076
  43.3 36.9 %copy-start.1 = (f32[1,2,1,1,102400]{4,3,2,1,0:T(1,128)S(1)}, f32[1,2,1,1,102400]{4,3,2,1,0:T(1,128)}, u32[]{:S(2)}) copy-start(f32[1,2,1,1,102400]{4,3,2,1,0:T(1,128)} %param.19) | copy-start | bytes 2457604
  92.0 33.4 %collective-permute-start.6 = (f32[3,100,128]{2,1,0:T(8,128)}, f32[3,100,128]{2,1,0:T(8,128)}, u32[]{:S(2)}, u32[]{:S(2)}) collective-permute-start(f32[3,100,128]{2,1,0:T(8,128)} %get-tuple-element.474), channel_id=1, source_target_pairs={{16,0},{32,16},{48,32},{64,48},{80,64},{96,80},{112,96},{17,1},{33... | collective-permute-start | bytes 460808 | tf_op jit(solution)/shard_map/ppermute | solution.py:39
  94.2 31.2 %collective-permute-start.5 = (f32[3,100,128]{2,1,0:T(8,128)}, f32[3,100,128]{2,1,0:T(8,128)}, u32[]{:S(2)}, u32[]{:S(2)}) collective-permute-start(f32[3,100,128]{2,1,0:T(8,128)} %get-tuple-element.475), channel_id=1, source_target_pairs={{0,16},{16,32},{32,48},{48,64},{64,80},{80,96},{96,112},{1,17},{17... | collective-permute-start | bytes 460808 | tf_op jit(solution)/shard_map/ppermute | solution.py:38
  97.0 28.3 %collective-permute-start.8 = (f32[3,800,1]{1,2,0:T(1,128)}, f32[3,800,1]{1,2,0:T(1,128)S(1)}, u32[]{:S(2)}, u32[]{:S(2)}) collective-permute-start(f32[3,800,1]{1,2,0:T(1,128)} %get-tuple-element.468), channel_id=1, source_target_pairs={{1,0},{2,1},{3,2},{4,3},{5,4},{6,5},{7,6},{8,7},{9,8},{10,9},{11,1... | collective-permute-start | bytes 28808 | tf_op jit(solution)/shard_map/ppermute | solution.py:41
  99.6 25.7 %collective-permute-start.7 = (f32[3,800,1]{1,2,0:T(1,128)}, f32[3,800,1]{1,2,0:T(1,128)}, u32[]{:S(2)}, u32[]{:S(2)}) collective-permute-start(f32[3,800,1]{1,2,0:T(1,128)} %get-tuple-element.469), channel_id=1, source_target_pairs={{0,1},{1,2},{2,3},{3,4},{4,5},{5,6},{6,7},{7,8},{8,9},{9,10},{10,1... | collective-permute-start | bytes 28808 | tf_op jit(solution)/shard_map/ppermute | solution.py:40
  136.8 36.3 %copy-start.2 = (f32[3,800,128]{2,1,0:T(8,128)S(1)}, f32[3,800,128]{2,1,0:T(8,128)}, u32[]{:S(2)}) copy-start(f32[3,800,128]{2,1,0:T(8,128)} %get-tuple-element.285) | copy-start | bytes 3686404
  139.8 33.3 %collective-permute-start.10 = (f32[3,100,128]{2,1,0:T(8,128)}, f32[3,100,128]{2,1,0:T(8,128)}, u32[]{:S(2)}, u32[]{:S(2)}) collective-permute-start(f32[3,100,128]{2,1,0:T(8,128)} %get-tuple-element.472), channel_id=1, source_target_pairs={{16,0},{32,16},{48,32},{64,48},{80,64},{96,80},{112,96},{17,1},{33... | collective-permute-start | bytes 460808 | tf_op jit(solution)/shard_map/ppermute | solution.py:39
  141.8 31.2 %collective-permute-start.9 = (f32[3,100,128]{2,1,0:T(8,128)}, f32[3,100,128]{2,1,0:T(8,128)}, u32[]{:S(2)}, u32[]{:S(2)}) collective-permute-start(f32[3,100,128]{2,1,0:T(8,128)} %get-tuple-element.473), channel_id=1, source_target_pairs={{0,16},{16,32},{32,48},{48,64},{64,80},{80,96},{96,112},{1,17},{17... | collective-permute-start | bytes 460808 | tf_op jit(solution)/shard_map/ppermute | solution.py:38
  144.7 28.4 %collective-permute-start.12 = (f32[3,800,1]{1,2,0:T(1,128)}, f32[3,800,1]{1,2,0:T(1,128)S(1)}, u32[]{:S(2)}, u32[]{:S(2)}) collective-permute-start(f32[3,800,1]{1,2,0:T(1,128)} %get-tuple-element.466), channel_id=1, source_target_pairs={{1,0},{2,1},{3,2},{4,3},{5,4},{6,5},{7,6},{8,7},{9,8},{10,9},{11,1... | collective-permute-start | bytes 28808 | tf_op jit(solution)/shard_map/ppermute | solution.py:41
  147.3 25.8 %collective-permute-start.11 = (f32[3,800,1]{1,2,0:T(1,128)}, f32[3,800,1]{1,2,0:T(1,128)}, u32[]{:S(2)}, u32[]{:S(2)}) collective-permute-start(f32[3,800,1]{1,2,0:T(1,128)} %get-tuple-element.467), channel_id=1, source_target_pairs={{0,1},{1,2},{2,3},{3,4},{4,5},{5,6},{6,7},{7,8},{8,9},{9,10},{10,1... | collective-permute-start | bytes 28808 | tf_op jit(solution)/shard_map/ppermute | solution.py:40
  184.8 36.2 %copy-start.3 = (f32[3,800,128]{2,1,0:T(8,128)S(1)}, f32[3,800,128]{2,1,0:T(8,128)}, u32[]{:S(2)}) copy-start(f32[3,800,128]{2,1,0:T(8,128)} %get-tuple-element.287) | copy-start | bytes 3686404
  187.7 33.2 %collective-permute-start.14 = (f32[3,100,128]{2,1,0:T(8,128)}, f32[3,100,128]{2,1,0:T(8,128)}, u32[]{:S(2)}, u32[]{:S(2)}) collective-permute-start(f32[3,100,128]{2,1,0:T(8,128)} %get-tuple-element.470), channel_id=1, source_target_pairs={{16,0},{32,16},{48,32},{64,48},{80,64},{96,80},{112,96},{17,1},{33... | collective-permute-start | bytes 460808 | tf_op jit(solution)/shard_map/ppermute | solution.py:39
  189.7 31.2 %collective-permute-start.13 = (f32[3,100,128]{2,1,0:T(8,128)}, f32[3,100,128]{2,1,0:T(8,128)}, u32[]{:S(2)}, u32[]{:S(2)}) collective-permute-start(f32[3,100,128]{2,1,0:T(8,128)} %get-tuple-element.471), channel_id=1, source_target_pairs={{0,16},{16,32},{32,48},{48,64},{64,80},{80,96},{96,112},{1,17},{17... | collective-permute-start | bytes 460808 | tf_op jit(solution)/shard_map/ppermute | solution.py:38
  192.6 28.3 %collective-permute-start.16 = (f32[3,800,1]{1,2,0:T(1,128)}, f32[3,800,1]{1,2,0:T(1,128)S(1)}, u32[]{:S(2)}, u32[]{:S(2)}) collective-permute-start(f32[3,800,1]{1,2,0:T(1,128)} %get-tuple-element.464), channel_id=1, source_target_pairs={{1,0},{2,1},{3,2},{4,3},{5,4},{6,5},{7,6},{8,7},{9,8},{10,9},{11,1... | collective-permute-start | bytes 28808 | tf_op jit(solution)/shard_map/ppermute | solution.py:41
  195.2 25.8 %collective-permute-start.15 = (f32[3,800,1]{1,2,0:T(1,128)}, f32[3,800,1]{1,2,0:T(1,128)}, u32[]{:S(2)}, u32[]{:S(2)}) collective-permute-start(f32[3,800,1]{1,2,0:T(1,128)} %get-tuple-element.465), channel_id=1, source_target_pairs={{0,1},{1,2},{2,3},{3,4},{4,5},{5,6},{6,7},{7,8},{8,9},{9,10},{10,1... | collective-permute-start | bytes 28808 | tf_op jit(solution)/shard_map/ppermute | solution.py:40
where the time goes:
time: 232 us; the launch traced here: 231 us
  Pallas kernels  117 us (50%)
  starting transfers between devices  53.8 us (23%)
  local copies, waits for them, and re-layouts  51.7 us (22%)
  other arithmetic  7.59 us (3%)
    pallas_call x4, Pallas kernels, exchange_tiles(): pl.pallas_call(functools.partial(exchange_kernel, (owners, columns)), out...  91.9 us
    pallas_call x4, Pallas kernels, run_step(): pl.pallas_call(kernel, out_shape=(jax.ShapeDtypeStruct((3, ROWS, CY), jnp...  24.7 us
    all_to_all x1, starting transfers between devices, route(): lax.all_to_all(tile_rows, ('gx', 'gy'), split_axis=0, concat_axis=0, tile...  16.1 us
    another operation x11, local copies, waits for them, and re-layouts  13.7 us
    ppermute x4, starting transfers between devices, exchange_halos(): low_y = lax.ppermute(current[:, :, CY - 1:], 'gy', forward_y)  13 us
    ppermute x4, starting transfers between devices, exchange_halos(): high_y = lax.ppermute(current[:, :, :1], 'gy', backward_y)  9.62 us
    ppermute x4, starting transfers between devices, exchange_halos(): high_x = lax.ppermute(current[:, :NL], 'gx', backward_x)  9.35 us
    cond x3, local copies, waits for them, and re-layouts, on_device(): updated, outgoing = lax.cond(section == 0, elastic_branch, shallow_branch)  7.38 us
  transfers between devices with their start and end apart: 18, of which 0 were waited for; matrix products, arithmetic and copies ran while one was open for 12% of the time, Pallas kernels for 40%

commit v1 on v0

--- a/solution.py
+++ b/solution.py
@@ -16,9 +16,10 @@
 
 ROWS = CX * NL
 BASE = 104
-PAD_ROWS = BASE + ROWS + NL + 8
+PAD_ROWS = BASE + ROWS + BASE
 CHUNK = 40
 EDGE = 16
+HALO_ROWS = NL + 4
 
 
 def from_partner(value, axis, stride):
@@ -33,20 +34,17 @@
 
 
 def exchange_halos(current):
-    forward_x, backward_x = shift_pairs("gx")
     forward_y, backward_y = shift_pairs("gy")
-    low_x = lax.ppermute(current[:, ROWS - NL :], "gx", forward_x)
-    high_x = lax.ppermute(current[:, :NL], "gx", backward_x)
     low_y = lax.ppermute(current[:, :, CY - 1 :], "gy", forward_y)
     high_y = lax.ppermute(current[:, :, :1], "gy", backward_y)
-    return low_x, high_x, low_y, high_y
+    return low_y, high_y
 
 
 def fill_scratch(scratch, cur_ref, low_ref, high_ref, fields):
     for f in range(fields):
-        scratch[f, pl.ds(BASE - NL, NL), :] = low_ref[f]
+        scratch[f, pl.ds(BASE - HALO_ROWS, HALO_ROWS), :] = low_ref[f]
         scratch[f, pl.ds(BASE, ROWS), :] = cur_ref[f]
-        scratch[f, pl.ds(BASE + ROWS, NL), :] = high_ref[f]
+        scratch[f, pl.ds(BASE + ROWS, HALO_ROWS), :] = high_ref[f]
 
 
 def lane_index(rows):
@@ -176,19 +174,52 @@
     )(*operands)
 
 
-def exchange_kernel(sizes, out_ref, in_ref, land, send_sem, recv_sem):
-    owners, columns = sizes
+def exchange_kernel(sizes, cur_ref, out_ref, in_ref, low_ref, high_ref, land, halo, send_sem, recv_sem,
+                    halo_send, halo_recv):
+    owners, rows_of, columns = sizes
     other = 1 - lax.axis_index("sec")
-    me = lax.axis_index("gx") * columns + lax.axis_index("gy")
+    section = lax.axis_index("sec")
+    gx = lax.axis_index("gx")
+    gy = lax.axis_index("gy")
+    me = gx * columns + gy
+    has_low = gx > 0
+    has_high = gx < rows_of - 1
+    halo[...] = jnp.zeros_like(halo)
     barrier = pltpu.get_barrier_semaphore()
-
     def greet(d, carry):
         pl.semaphore_signal(barrier, inc=1, device_id=(other, d // columns, d % columns),
                             device_id_type=pl.DeviceIdType.MESH)
         return carry
 
-    lax.fori_loop(0, owners, greet, 0)
-    pl.semaphore_wait(barrier, owners)
+    lax.fori_loop(0, owners, greet, 0, unroll=8)
+
+    @pl.when(has_low)
+    def _():
+        pl.semaphore_signal(barrier, inc=1, device_id=(section, gx - 1, gy), device_id_type=pl.DeviceIdType.MESH)
+
+    @pl.when(has_high)
+    def _():
+        pl.semaphore_signal(barrier, inc=1, device_id=(section, gx + 1, gy), device_id_type=pl.DeviceIdType.MESH)
+
+    pl.semaphore_wait(barrier, owners + has_low.astype(jnp.int32) + has_high.astype(jnp.int32))
+
+    def slab_copy(start, slot, target):
+        return pltpu.make_async_remote_copy(
+            src_ref=cur_ref.at[:, pl.ds(start, HALO_ROWS), :],
+            dst_ref=halo.at[slot],
+            send_sem=halo_send.at[slot],
+            recv_sem=halo_recv.at[slot],
+            device_id=(section, target, gy),
+            device_id_type=pl.DeviceIdType.MESH,
+        )
+
+    @pl.when(has_high)
+    def _():
+        slab_copy(ROWS - HALO_ROWS, 0, gx + 1).start()
+
+    @pl.when(has_low)
+    def _():
+        slab_copy(0, 1, gx - 1).start()
 
     def send(d, carry):
         pltpu.make_async_remote_copy(
@@ -201,33 +232,50 @@
         ).start()
         return carry
 
-    lax.fori_loop(0, owners, send, 0)
+    lax.fori_loop(0, owners, send, 0, unroll=8)
     whole = pltpu.make_async_remote_copy(
         src_ref=out_ref,
         dst_ref=land,
         send_sem=send_sem,
         recv_sem=recv_sem,
-        device_id=(other, lax.axis_index("gx"), lax.axis_index("gy")),
+        device_id=(other, gx, gy),
         device_id_type=pl.DeviceIdType.MESH,
     )
+
+    @pl.when(has_high)
+    def _():
+        slab_copy(ROWS - HALO_ROWS, 0, gx + 1).wait_send()
+        slab_copy(0, 1, gx + 1).wait_recv()
+
+    @pl.when(has_low)
+    def _():
+        slab_copy(0, 1, gx - 1).wait_send()
+        slab_copy(ROWS - HALO_ROWS, 0, gx - 1).wait_recv()
+
     whole.wait_send()
     whole.wait_recv()
     in_ref[...] = land[...]
-
-
-def exchange_tiles(outgoing, owners, columns):
+    low_ref[...] = halo[0]
+    high_ref[...] = halo[1]
+
+
+def exchange(current, outgoing, owners, rows_of, columns):
+    halo_shape = jax.ShapeDtypeStruct((3, HALO_ROWS, CY), jnp.float32)
     return pl.pallas_call(
-        functools.partial(exchange_kernel, (owners, columns)),
-        out_shape=jax.ShapeDtypeStruct(outgoing.shape, jnp.float32),
-        in_specs=vmem_specs(1),
-        out_specs=pl.BlockSpec(memory_space=pltpu.VMEM),
+        functools.partial(exchange_kernel, (owners, rows_of, columns)),
+        out_shape=(jax.ShapeDtypeStruct(outgoing.shape, jnp.float32), halo_shape, halo_shape),
+        in_specs=[pl.BlockSpec(memory_space=pl.ANY), pl.BlockSpec(memory_space=pltpu.VMEM)],
+        out_specs=tuple(vmem_specs(3)),
         scratch_shapes=[
             pltpu.VMEM(outgoing.shape, jnp.float32),
+            pltpu.VMEM((2, 3, HALO_ROWS, CY), jnp.float32),
             pltpu.SemaphoreType.DMA(()),
             pltpu.SemaphoreType.DMA(()),
+            pltpu.SemaphoreType.DMA((2,)),
+            pltpu.SemaphoreType.DMA((2,)),
         ],
         compiler_params=pltpu.CompilerParams(collective_id=0, has_side_effects=True),
-    )(outgoing)
+    )(current, outgoing)
 
 
 def route(payload):
@@ -279,8 +327,8 @@
     outgoing = jnp.zeros((owners * CAP, CY), jnp.float32).at[position].set(picked * weights[:, None])
     arrived_rows = deliver(jnp.zeros((owners, CAP, CY), jnp.float32), send_rows)[1].reshape(1, -1)
     for step_index in range(STEPS):
-        low_x, high_x, low_y, high_y = exchange_halos(current)
-        arrived = exchange_tiles(outgoing, owners, lax.axis_size("gy"))
+        low_y, high_y = exchange_halos(current)
+        arrived, low_x, high_x = exchange(current, outgoing, owners, lax.axis_size("gx"), lax.axis_size("gy"))
 
         def elastic_branch():
             scratch = [pltpu.VMEM((3, PAD_ROWS, CY), jnp.float32)]

time: 232 us -> 200 us (0.86)
  starting transfers between devices: 53.8 us -> 38.6 us
  Pallas kernels: 117 us -> 105 us
  local copies, waits for them, and re-layouts: 51.7 us -> 47.5 us
    ppermute x8 -> x0, starting transfers between devices: 14.5 us -> none  [the longest x4 9.35 us: exchange_halos(): high_x = lax.ppermute(current[:, :NL], 'gx', backward_x)]
    pallas_call x4, Pallas kernels: 91.9 us -> 80.2 us  [exchange(): pl.pallas_call(functools.partial(exchange_kernel, (owners, rows_of, colum...]
    slice x5 -> x1, local copies, waits for them, and re-layouts: 6.76 us -> 0.76 us  [on_device(): landing = pairs[:, 1]]
  transfers between devices with their start and end apart: 18 -> 10, of which waited for: 0 -> 0; matrix products, arithmetic and copies ran while one was open for 12% -> 12% of each run, Pallas kernels for 40% -> 40%
where the time goes in v1:
time: 200 us; the launch traced here: 199 us
  Pallas kernels  105 us (52%)
  local copies, waits for them, and re-layouts  47.5 us (24%)
  starting transfers between devices  38.6 us (19%)
  other arithmetic  6.98 us (3%)
    pallas_call x4, Pallas kernels, exchange(): pl.pallas_call(functools.partial(exchange_kernel, (owners, rows_of, colum...  80.2 us
    pallas_call x4, Pallas kernels, run_step(): pl.pallas_call(kernel, out_shape=(jax.ShapeDtypeStruct((3, ROWS, CY), jnp...  24.8 us
    all_to_all x1, starting transfers between devices, route(): lax.all_to_all(tile_rows, ('gx', 'gy'), split_axis=0, concat_axis=0, tile...  16.1 us
    another operation x11, local copies, waits for them, and re-layouts  13.9 us
    ppermute x4, starting transfers between devices, exchange_halos(): low_y = lax.ppermute(current[:, :, CY - 1:], 'gy', forward_y)  12.9 us
    ppermute x4, starting transfers between devices, exchange_halos(): high_y = lax.ppermute(current[:, :, :1], 'gy', backward_y)  8.97 us
    slice x5, local copies, waits for them, and re-layouts, exchange_halos(): high_y = lax.ppermute(current[:, :, :1], 'gy', backward_y)  8.78 us
    cond x3, local copies, waits for them, and re-layouts, on_device(): updated, outgoing = lax.cond(section == 0, elastic_branch, shallow_branch)  7.35 us
  transfers between devices with their start and end apart: 10, of which 0 were waited for; matrix products, arithmetic and copies ran while one was open for 12% of the time, Pallas kernels for 40%

profile of v1, /device:TPU:31, one launch (start us, length us, event | category | flops | bytes accessed | tf_op | source)
XLA Modules:
  0.0 198.9 jit_solution(7206556498462264925)
XLA Ops:
  1.8 0.9 fusion.3
  3.4 1.4 scatter_custom_fusion.1
  5.5 16.1 %all-to-all-start = ((s32[128,1,4]{2,1,0:T(1,128)}), s32[128,1,4]{2,1,0:T(1,128)S(1)}, u32[]{:S(2)}, u32[]{:S(2)}) async-start(s32[128,1,4]{2,1,0:T(1,128)} %bitcast.19), calls=%async_computation | async-start | bytes 131072 | tf_op jit(solution)/shard_map/all_to_all | solution.py:286
  21.6 3.1 %fusion.19 = (f32[3,800,1]{2,1,0:T(8,128)S(1)}, f32[3,800,1]{2,1,0:T(8,128)}) fusion(f32[3,800,128]{2,1,0:T(8,128)} %bitcast.43), kind=kLoop, calls=%fused_computation.38 | loop fusion | bytes 38400 | tf_op jit(solution)/shard_map/slice | solution.py:39
  24.8 2.4 %copy.23 = f32[3,800,1]{1,2,0:T(1,128)} copy(f32[3,800,1]{2,1,0:T(8,128)} %get-tuple-element.407) | data formatting | bytes 19200 | tf_op jit(solution)/shard_map/slice | solution.py:38
  27.2 3.3 %collective-permute-start = (f32[3,800,1]{1,2,0:T(1,128)}, f32[3,800,1]{1,2,0:T(1,128)S(1)}, u32[]{:S(2)}, u32[]{:S(2)}) collective-permute-start(f32[3,800,1]{1,2,0:T(1,128)} %copy.23), channel_id=1, source_target_pairs={{0,1},{1,2},{2,3},{3,4},{4,5},{5,6},{6,7},{7,8},{8,9},{9,10},{10,1... | collective-permute-start | bytes 28808 | tf_op jit(solution)/shard_map/ppermute | solution.py:38
  30.5 1.0 copy.24
  31.5 1.9 collective-permute-start.1
  33.5 1.6 scatter_custom_fusion.3
  35.0 1.4 scatter_custom_fusion.2
  38.7 9.9 %conditional.5 = (f32[256,128]{1,0:T(8,128)S(1)}) conditional(s32[]{:T(128)} %convert_element_type.14, (f32[3,800,128]{2,1,0:T(8,128)S(1)}, s32[256]{0:T(256)S(1)}) %tuple.113, (f32[3,800,128]{2,1,0:T(8,128)S(1)}, s32[256]{0:T(256)S(1)}) %tuple.114), branch_computations={%region_3.5_spmd, %region_5.6_spmd} | conditional | flops 329472 | bytes 11477004 | solution.py:326
  38.8 2.3 %gather_fusion = f32[256,1280]{1,0:T(8,128)} fusion(f32[80,1280]{1,0:T(8,128)S(1)} %squeeze.10, s32[1024]{0:T(1024)S(1)} %pad_clamp_fusion), kind=kCustom, calls=%fused_computation | custom fusion | bytes 2622464 | tf_op jit(solution)/shard_map/cond/branch_0_fun/gather | solution.py:323
  41.1 2.8 %copy.17 = f32[256,1280]{0,1:T(8,128)} copy(f32[256,1280]{1,0:T(8,128)} %gather_fusion) | data formatting | bytes 2621440 | tf_op jit(solution)/shard_map/cond/branch_0_fun/gather | solution.py:323
  43.9 2.6 %reshape.64 = f32[256,128,10]{0,2,1:T(8,128)} reshape(f32[256,1280]{0,1:T(8,128)} %copy.17) | data formatting | bytes 2621440 | tf_op jit(solution)/shard_map/cond/branch_0_fun/reshape | solution.py:324
  46.5 2.0 reduce_sum.9
  48.6 2.2 %scatter_custom_fusion.out_ref = f32[512,128]{1,0:T(8,128)} fusion(s32[256]{0:T(256)} %bitcast.88, f32[256,128]{1,0:T(8,128)S(1)} %get-tuple-element.398, f32[]{:T(128)} %constant.22.clone.1, f32[256]{0:T(256)S(1)} %bitcast.84), kind=kCustom, calls=%fused_computation.18 | custom fusion | flops 32768 | bytes 394752 | tf_op jit(solution)/shard_map/scatter | solution.py:327
  50.8 21.6 %shard_map.75 = (f32[512,128]{1,0:T(8,128)}, f32[3,104,128]{2,1,0:T(8,128)}, f32[3,104,128]{2,1,0:T(8,128)}) custom-call(f32[3,800,128]{2,1,0:T(8,128)S(1)} %bitcast.46, f32[512,128]{1,0:T(8,128)} %scatter_custom_fusion.out_ref), custom_call_target="tpu_custom_call" | custom-call | tf_op jit(solution)/shard_map/pallas_call | solution.py:264
  72.4 9.6 %conditional.6 = ((f32[3,800,128]{2,1,0:T(8,128)S(1)}, f32[512,128]{1,0:T(8,128)})) conditional(s32[]{:T(128)} %convert_element_type.14, (f32[3,800,128]{2,1,0:T(8,128)S(1)}, f32[3,800,128]{2,1,0:T(8,128)}, f32[2,800,128]{2,1,0:T(8,128)S(1)}, s32[800,128]{1,0:T(8,128)}, f32[3,104,128]{2,1,0:T(8,128)}, /*index=5*/f32[3,104,128]{2,1,0:T(8,128)}, ...), branch_computations={%region_10.11_spmd, %region_11.12_spmd} | conditional | bytes 38408 | solution.py:348
  72.6 1.5 copy.27.right_ref
  74.1 1.4 copy.26.left_ref
  75.5 6.4 %branch_0_fun.4 = (f32[3,800,128]{2,1,0:T(8,128)S(1)}, f32[512,128]{1,0:T(8,128)}) custom-call(f32[3,800,128]{2,1,0:T(8,128)S(1)} %get-tuple-element.191.cur_ref, f32[3,800,128]{2,1,0:T(8,128)} %get-tuple-element.192.prev_ref, f32[2,800,128]{2,1,0:T(8,128)S(1)} %get-tuple-element.193.coef_ref, s32[800,128]{1,0:T(8,128)} %get-tuple-element.194.wet_ref, ...), custom_call_target="tpu_custom_call" | custom-call | tf_op jit(solution)/shard_map/cond/branch_0_fun/pallas_call | solution.py:165
  81.9 1.5 copy.30
  83.5 1.5 fusion.18
  85.0 2.5 %collective-permute-start.4 = (f32[3,800,1]{1,2,0:T(1,128)}, f32[3,800,1]{1,2,0:T(1,128)S(1)}, u32[]{:S(2)}, u32[]{:S(2)}) collective-permute-start(f32[3,800,1]{1,2,0:T(1,128)} %get-tuple-element.404), channel_id=1, source_target_pairs={{1,0},{2,1},{3,2},{4,3},{5,4},{6,5},{7,6},{8,7},{9,8},{10,9},{11,1... | collective-permute-start | bytes 28808 | tf_op jit(solution)/shard_map/ppermute | solution.py:39
  87.5 3.1 %collective-permute-start.3 = (f32[3,800,1]{1,2,0:T(1,128)}, f32[3,800,1]{1,2,0:T(1,128)}, u32[]{:S(2)}, u32[]{:S(2)}) collective-permute-start(f32[3,800,1]{1,2,0:T(1,128)} %get-tuple-element.405), channel_id=1, source_target_pairs={{0,1},{1,2},{2,3},{3,4},{4,5},{5,6},{6,7},{7,8},{8,9},{9,10},{10,1... | collective-permute-start | bytes 28808 | tf_op jit(solution)/shard_map/ppermute | solution.py:38
  90.6 19.1 %shard_map.76 = (f32[512,128]{1,0:T(8,128)}, f32[3,104,128]{2,1,0:T(8,128)}, f32[3,104,128]{2,1,0:T(8,128)}) custom-call(f32[3,800,128]{2,1,0:T(8,128)S(1)} %get-tuple-element.298.cur_ref, f32[512,128]{1,0:T(8,128)} %get-tuple-element.299.out_ref), custom_call_target="tpu_custom_call" | custom-call | tf_op jit(solution)/shard_map/pallas_call | solution.py:264
  109.7 9.8 %conditional.7 = ((f32[3,800,128]{2,1,0:T(8,128)}, f32[512,128]{1,0:T(8,128)})) conditional(s32[]{:T(128)} %convert_element_type.14, (f32[3,800,128]{2,1,0:T(8,128)S(1)}, f32[3,800,128]{2,1,0:T(8,128)S(1)}, f32[2,800,128]{2,1,0:T(8,128)S(1)}, s32[800,128]{1,0:T(8,128)}, f32[3,104,128]{2,1,0:T(8,128)}, /*index=5*/f32[3,104,128]{2,1,0:T(8,128)}, ...), branch_computations={%region_12.13_spmd, %region_13.14_spmd} | conditional | bytes 38408 | solution.py:348
  109.7 1.5 copy.33.right_ref
  111.2 2.2 %copy.32.left_ref = f32[3,800,1]{2,1,0:T(8,128)} copy(f32[3,800,1]{1,2,0:T(1,128)} %get-tuple-element.341) | data formatting | bytes 19200 | tf_op jit(solution)/shard_map
  113.4 6.1 %branch_0_fun.5 = (f32[3,800,128]{2,1,0:T(8,128)}, f32[512,128]{1,0:T(8,128)}) custom-call(f32[3,800,128]{2,1,0:T(8,128)S(1)} %get-tuple-element.212.cur_ref, f32[3,800,128]{2,1,0:T(8,128)S(1)} %get-tuple-element.213.prev_ref, f32[2,800,128]{2,1,0:T(8,128)S(1)} %get-tuple-element.214.coef_ref, s32[800,128]{1,0:T(8,128)} %get-tuple-element.215.wet_ref, ...), custom_call_target="tpu_custom_call" | custom-call | tf_op jit(solution)/shard_map/cond/branch_0_fun/pallas_call | solution.py:165
  119.5 2.9 %copy.36 = f32[3,800,128]{1,2,0:T(8,128)} copy(f32[3,800,128]{2,1,0:T(8,128)} %get-tuple-element.303.cur_ref) | data formatting | bytes 2457600 | tf_op jit(solution)/shard_map/cond | solution.py:348
  122.4 1.5 fusion.17
  123.9 2.3 %collective-permute-start.6 = (f32[3,800,1]{1,2,0:T(1,128)}, f32[3,800,1]{1,2,0:T(1,128)S(1)}, u32[]{:S(2)}, u32[]{:S(2)}) collective-permute-start(f32[3,800,1]{1,2,0:T(1,128)} %get-tuple-element.402), channel_id=1, source_target_pairs={{1,0},{2,1},{3,2},{4,3},{5,4},{6,5},{7,6},{8,7},{9,8},{10,9},{11,1... | collective-permute-start | bytes 28808 | tf_op jit(solution)/shard_map/ppermute | solution.py:39
  126.2 3.3 %collective-permute-start.5 = (f32[3,800,1]{1,2,0:T(1,128)}, f32[3,800,1]{1,2,0:T(1,128)}, u32[]{:S(2)}, u32[]{:S(2)}) collective-permute-start(f32[3,800,1]{1,2,0:T(1,128)} %get-tuple-element.403), channel_id=1, source_target_pairs={{0,1},{1,2},{2,3},{3,4},{4,5},{5,6},{6,7},{7,8},{8,9},{9,10},{10,1... | collective-permute-start | bytes 28808 | tf_op jit(solution)/shard_map/ppermute | solution.py:38
  129.5 19.6 %shard_map.77 = (f32[512,128]{1,0:T(8,128)}, f32[3,104,128]{2,1,0:T(8,128)}, f32[3,104,128]{2,1,0:T(8,128)}) custom-call(f32[3,800,128]{2,1,0:T(8,128)S(1)} %copy-done.2, f32[512,128]{1,0:T(8,128)} %get-tuple-element.304.out_ref), custom_call_target="tpu_custom_call" | custom-call | tf_op jit(solution)/shard_map/pallas_call | solution.py:264
  149.1 10.0 %conditional.8 = ((f32[3,800,128]{2,1,0:T(8,128)}, f32[512,128]{1,0:T(8,128)})) conditional(s32[]{:T(128)} %convert_element_type.14, (f32[3,800,128]{2,1,0:T(8,128)S(1)}, f32[3,800,128]{2,1,0:T(8,128)S(1)}, f32[2,800,128]{2,1,0:T(8,128)S(1)}, s32[800,128]{1,0:T(8,128)}, f32[3,104,128]{2,1,0:T(8,128)}, /*index=5*/f32[3,104,128]{2,1,0:T(8,128)}, ...), branch_computations={%region_14.15_spmd, %region_15.16_spmd} | conditional | bytes 38408 | solution.py:348
  149.3 1.5 copy.39.right_ref
  150.8 2.2 %copy.38.left_ref = f32[3,800,1]{2,1,0:T(8,128)} copy(f32[3,800,1]{1,2,0:T(1,128)} %get-tuple-element.362) | data formatting | bytes 19200 | tf_op jit(solution)/shard_map
  153.0 6.1 %branch_0_fun.6 = (f32[3,800,128]{2,1,0:T(8,128)}, f32[512,128]{1,0:T(8,128)}) custom-call(f32[3,800,128]{2,1,0:T(8,128)S(1)} %get-tuple-element.233.cur_ref, f32[3,800,128]{2,1,0:T(8,128)S(1)} %get-tuple-element.234.prev_ref, f32[2,800,128]{2,1,0:T(8,128)S(1)} %get-tuple-element.235.coef_ref, s32[800,128]{1,0:T(8,128)} %get-tuple-element.236.wet_ref, ...), custom_call_target="tpu_custom_call" | custom-call | tf_op jit(solution)/shard_map/cond/branch_0_fun/pallas_call | solution.py:165
  159.1 2.9 %copy.42 = f32[3,800,128]{1,2,0:T(8,128)} copy(f32[3,800,128]{2,1,0:T(8,128)} %get-tuple-element.308.cur_ref) | data formatting | bytes 2457600 | tf_op jit(solution)/shard_map/cond | solution.py:348
  162.0 1.5 fusion.16
  163.6 2.3 %collective-permute-start.8 = (f32[3,800,1]{1,2,0:T(1,128)}, f32[3,800,1]{1,2,0:T(1,128)S(1)}, u32[]{:S(2)}, u32[]{:S(2)}) collective-permute-start(f32[3,800,1]{1,2,0:T(1,128)} %get-tuple-element.400), channel_id=1, source_target_pairs={{1,0},{2,1},{3,2},{4,3},{5,4},{6,5},{7,6},{8,7},{9,8},{10,9},{11,1... | collective-permute-start | bytes 28808 | tf_op jit(solution)/shard_map/ppermute | solution.py:39
  165.9 3.3 %collective-permute-start.7 = (f32[3,800,1]{1,2,0:T(1,128)}, f32[3,800,1]{1,2,0:T(1,128)}, u32[]{:S(2)}, u32[]{:S(2)}) collective-permute-start(f32[3,800,1]{1,2,0:T(1,128)} %get-tuple-element.401), channel_id=1, source_target_pairs={{0,1},{1,2},{2,3},{3,4},{4,5},{5,6},{6,7},{7,8},{8,9},{9,10},{10,1... | collective-permute-start | bytes 28808 | tf_op jit(solution)/shard_map/ppermute | solution.py:38
  169.1 20.0 %shard_map.78 = (f32[512,128]{1,0:T(8,128)}, f32[3,104,128]{2,1,0:T(8,128)}, f32[3,104,128]{2,1,0:T(8,128)}) custom-call(f32[3,800,128]{2,1,0:T(8,128)S(1)} %copy-done.3, f32[512,128]{1,0:T(8,128)} %get-tuple-element.309.out_ref), custom_call_target="tpu_custom_call" | custom-call | tf_op jit(solution)/shard_map/pallas_call | solution.py:264
  189.1 9.8 %conditional.9 = (f32[1,3,1,1,102400]{4,3,2,1,0:T(1,128)}) conditional(s32[]{:T(128)} %convert_element_type.14, (f32[3,800,128]{2,1,0:T(8,128)S(1)}, f32[3,800,128]{2,1,0:T(8,128)S(1)}, f32[2,800,128]{2,1,0:T(8,128)S(1)}, s32[800,128]{1,0:T(8,128)}, f32[3,104,128]{2,1,0:T(8,128)}, /*index=5*/f32[3,104,128]{2,1,0:T(8,128)}, ...), branch_computations={%region_16.17_spmd, %region_17.18_spmd} | conditional | bytes 38408 | solution.py:348
  189.2 1.5 copy.45.right_ref
  190.6 2.2 %copy.44.left_ref = f32[3,800,1]{2,1,0:T(8,128)} copy(f32[3,800,1]{1,2,0:T(1,128)} %get-tuple-element.383) | data formatting | bytes 19200 | tf_op jit(solution)/shard_map
  192.8 6.1 %branch_0_fun.7 = (f32[3,800,128]{2,1,0:T(8,128)}, f32[512,128]{1,0:T(8,128)}) custom-call(f32[3,800,128]{2,1,0:T(8,128)S(1)} %get-tuple-element.254.cur_ref, f32[3,800,128]{2,1,0:T(8,128)S(1)} %get-tuple-element.255.prev_ref, f32[2,800,128]{2,1,0:T(8,128)S(1)} %get-tuple-element.256.coef_ref, s32[800,128]{1,0:T(8,128)} %get-tuple-element.257.wet_ref, ...), custom_call_target="tpu_custom_call" | custom-call | tf_op jit(solution)/shard_map/cond/branch_0_fun/pallas_call | solution.py:165
  (44 shorter events, 5.7 us)
Async XLA Ops:
  3.4 31.6 %copy-start.5 = (s32[256,1]{0,1:T(1,128)}, s32[256,1]{0,1:T(1,128)S(1)}, u32[]{:S(2)}) copy-start(s32[256,1]{0,1:T(1,128)S(1)} %compare_select_fusion.2) | copy-start | bytes 3076
  5.5 30.9 %all-to-all-start = ((s32[128,1,4]{2,1,0:T(1,128)}), s32[128,1,4]{2,1,0:T(1,128)S(1)}, u32[]{:S(2)}, u32[]{:S(2)}) async-start(s32[128,1,4]{2,1,0:T(1,128)} %bitcast.19), calls=%async_computation | async-start | bytes 131072 | tf_op jit(solution)/shard_map/all_to_all | solution.py:286
  24.8 13.9 %copy-start = (f32[1,3,1,1,102400]{4,3,2,1,0:T(1,128)S(1)}, f32[1,3,1,1,102400]{4,3,2,1,0:T(1,128)}, u32[]{:S(2)}) copy-start(f32[1,3,1,1,102400]{4,3,2,1,0:T(1,128)} %param.17) | copy-start | bytes 3686404
  27.2 45.2 %collective-permute-start = (f32[3,800,1]{1,2,0:T(1,128)}, f32[3,800,1]{1,2,0:T(1,128)S(1)}, u32[]{:S(2)}, u32[]{:S(2)}) collective-permute-start(f32[3,800,1]{1,2,0:T(1,128)} %copy.23), channel_id=1, source_target_pairs={{0,1},{1,2},{2,3},{3,4},{4,5},{5,6},{6,7},{7,8},{8,9},{9,10},{10,1... | collective-permute-start | bytes 28808 | tf_op jit(solution)/shard_map/ppermute | solution.py:38
  31.5 40.8 %collective-permute-start.1 = (f32[3,800,1]{1,2,0:T(1,128)}, f32[3,800,1]{1,2,0:T(1,128)S(1)}, u32[]{:S(2)}, u32[]{:S(2)}) collective-permute-start(f32[3,800,1]{1,2,0:T(1,128)} %copy.24), channel_id=1, source_target_pairs={{1,0},{2,1},{3,2},{4,3},{5,4},{6,5},{7,6},{8,7},{9,8},{10,9},{11,1... | collective-permute-start | bytes 28808 | tf_op jit(solution)/shard_map/ppermute | solution.py:39
  37.9 34.5 %collective-permute-start.2 = (s32[512]{0:T(512)S(1)}, s32[512]{0:T(512)S(1)}, u32[]{:S(2)}, u32[]{:S(2)}) collective-permute-start(s32[512]{0:T(512)S(1)} %reshape.72), channel_id=1, source_target_pairs={{0,128},{128,0},{1,129},{129,1},{2,130},{130,2},{3,131},{131,3},{4... | collective-permute-start | bytes 6152 | tf_op jit(solution)/shard_map/ppermute | solution.py:26
  38.7 9.9 %copy-start.4 = (f32[1,1,1,256]{3,2,1,0:T(1,128)S(1)}, f32[1,1,1,256]{3,2,1,0:T(1,128)}, u32[]{:S(2)}) copy-start(f32[1,1,1,256]{3,2,1,0:T(1,128)} %param.23) | copy-start | bytes 3076
  48.6 23.8 %copy-start.1 = (f32[1,2,1,1,102400]{4,3,2,1,0:T(1,128)S(1)}, f32[1,2,1,1,102400]{4,3,2,1,0:T(1,128)}, u32[]{:S(2)}) copy-start(f32[1,2,1,1,102400]{4,3,2,1,0:T(1,128)} %param.19) | copy-start | bytes 2457604
  85.0 24.7 %collective-permute-start.4 = (f32[3,800,1]{1,2,0:T(1,128)}, f32[3,800,1]{1,2,0:T(1,128)S(1)}, u32[]{:S(2)}, u32[]{:S(2)}) collective-permute-start(f32[3,800,1]{1,2,0:T(1,128)} %get-tuple-element.404), channel_id=1, source_target_pairs={{1,0},{2,1},{3,2},{4,3},{5,4},{6,5},{7,6},{8,7},{9,8},{10,9},{11,1... | collective-permute-start | bytes 28808 | tf_op jit(solution)/shard_map/ppermute | solution.py:39
  87.5 22.2 %collective-permute-start.3 = (f32[3,800,1]{1,2,0:T(1,128)}, f32[3,800,1]{1,2,0:T(1,128)}, u32[]{:S(2)}, u32[]{:S(2)}) collective-permute-start(f32[3,800,1]{1,2,0:T(1,128)} %get-tuple-element.405), channel_id=1, source_target_pairs={{0,1},{1,2},{2,3},{3,4},{4,5},{5,6},{6,7},{7,8},{8,9},{9,10},{10,1... | collective-permute-start | bytes 28808 | tf_op jit(solution)/shard_map/ppermute | solution.py:38
  119.5 10.0 %copy-start.2 = (f32[3,800,128]{2,1,0:T(8,128)S(1)}, f32[3,800,128]{2,1,0:T(8,128)}, u32[]{:S(2)}) copy-start(f32[3,800,128]{2,1,0:T(8,128)} %get-tuple-element.303.cur_ref) | copy-start | bytes 3686404
  123.9 25.2 %collective-permute-start.6 = (f32[3,800,1]{1,2,0:T(1,128)}, f32[3,800,1]{1,2,0:T(1,128)S(1)}, u32[]{:S(2)}, u32[]{:S(2)}) collective-permute-start(f32[3,800,1]{1,2,0:T(1,128)} %get-tuple-element.402), channel_id=1, source_target_pairs={{1,0},{2,1},{3,2},{4,3},{5,4},{6,5},{7,6},{8,7},{9,8},{10,9},{11,1... | collective-permute-start | bytes 28808 | tf_op jit(solution)/shard_map/ppermute | solution.py:39
  126.2 22.9 %collective-permute-start.5 = (f32[3,800,1]{1,2,0:T(1,128)}, f32[3,800,1]{1,2,0:T(1,128)}, u32[]{:S(2)}, u32[]{:S(2)}) collective-permute-start(f32[3,800,1]{1,2,0:T(1,128)} %get-tuple-element.403), channel_id=1, source_target_pairs={{0,1},{1,2},{2,3},{3,4},{4,5},{5,6},{6,7},{7,8},{8,9},{9,10},{10,1... | collective-permute-start | bytes 28808 | tf_op jit(solution)/shard_map/ppermute | solution.py:38
  159.1 10.0 %copy-start.3 = (f32[3,800,128]{2,1,0:T(8,128)S(1)}, f32[3,800,128]{2,1,0:T(8,128)}, u32[]{:S(2)}) copy-start(f32[3,800,128]{2,1,0:T(8,128)} %get-tuple-element.308.cur_ref) | copy-start | bytes 3686404
  163.6 25.6 %collective-permute-start.8 = (f32[3,800,1]{1,2,0:T(1,128)}, f32[3,800,1]{1,2,0:T(1,128)S(1)}, u32[]{:S(2)}, u32[]{:S(2)}) collective-permute-start(f32[3,800,1]{1,2,0:T(1,128)} %get-tuple-element.400), channel_id=1, source_target_pairs={{1,0},{2,1},{3,2},{4,3},{5,4},{6,5},{7,6},{8,7},{9,8},{10,9},{11,1... | collective-permute-start | bytes 28808 | tf_op jit(solution)/shard_map/ppermute | solution.py:39
  165.9 23.3 %collective-permute-start.7 = (f32[3,800,1]{1,2,0:T(1,128)}, f32[3,800,1]{1,2,0:T(1,128)}, u32[]{:S(2)}, u32[]{:S(2)}) collective-permute-start(f32[3,800,1]{1,2,0:T(1,128)} %get-tuple-element.401), channel_id=1, source_target_pairs={{0,1},{1,2},{2,3},{3,4},{4,5},{5,6},{6,7},{7,8},{8,9},{9,10},{10,1... | collective-permute-start | bytes 28808 | tf_op jit(solution)/shard_map/ppermute | solution.py:38
